TPU v7x, 512 devices: a whole 4x4x16 slice. The times are simulated.
512 devices in a mesh: ctx: 64 (over z, x_lo, core), head: 8 (over y, x_hi).
Axes of the slice: x: 4 (x_hi: 2, x_lo: 2; x = x_hi * 2 + x_lo), y: 4, z: 16, core: 2. Of those that a mesh axis runs over, the one named last changes fastest.
Arguments:
- queries: bfloat16 [65536, 4096], P(('ctx', 'head')), may hold values from -6 to 6
- keys: bfloat16 [65536, 1024], P(('ctx', 'head')), may hold values from -6 to 6
- values: bfloat16 [65536, 1024], P(('ctx', 'head')), may hold values from -1.5 to 1.5
- out_grad: bfloat16 [65536, 4096], P(('ctx', 'head')), may hold values from -6 to 6
- log_norm: float32 [65536, 32], P(('ctx', 'head')), may hold values from 2 to 4
- row_delta: float32 [65536, 32], P(('ctx', 'head')), may hold values from -10 to 10
- tile_pairs: int32 [64, 4, 16, 2], P('ctx'), may hold values from 0 to 7, as said below
- pair_count: int32 [64, 4], P('ctx'), may hold values from 0 to 16, as said below
Outputs:
- query_grad: bfloat16 [65536, 4096], P(('ctx', 'head'))
- key_grad: bfloat16 [65536, 1024], P(('ctx', 'head'))
- value_grad: bfloat16 [65536, 1024], P(('ctx', 'head'))
Inputs may be any that keep to these rules, and one draw needn't show every extreme that they name: `tile_pairs`: Entries past pair_count are not read.
All inputs are finite; a program needn't handle non-finite values.
Results may differ from a plain program's by a relative error of at most 0.005.
Values may be sent and summed in bfloat16 or wider, within the bound.
A program may use at most 64 MiB of HBM per device.

v0:
```python
import functools

import jax
import jax.numpy as jnp
from jax import lax
from jax.experimental import pallas as pl
from jax.experimental.pallas import tpu as pltpu
from jax.sharding import PartitionSpec as P

HEAD_DIM = 128
TILE = 128
TPB = 8
WIN = 4
SLOTS = 16
GROUP = 4
WIDTH = GROUP * HEAD_DIM
SCALE = HEAD_DIM ** (-0.5)
LOG2E = 1.4426950408889634
MESH = pl.DeviceIdType.MESH


def wrap(value, size):
    return lax.rem(value + size, size)


def greet(ctx, head):
    n_ctx, n_head = lax.axis_size("ctx"), lax.axis_size("head")
    barrier = pltpu.get_barrier_semaphore()
    for d in range(1, n_head):
        pl.semaphore_signal(
            barrier, inc=1, device_id=(ctx, wrap(head + d, n_head)), device_id_type=MESH
        )
    for s in range(1, WIN):
        for there in (wrap(ctx + s, n_ctx), wrap(ctx - s, n_ctx)):
            pl.semaphore_signal(barrier, inc=1, device_id=(there, head), device_id_type=MESH)
    pl.semaphore_wait(barrier, n_head - 1 + 2 * (WIN - 1))


def gather_kernel(
    q_in, g_in, k_in, v_in, nd_in, q_out, g_out, k_out, v_out, nd_out,
    q_tmp, g_tmp, k_tmp, v_tmp, nd_tmp, send, recv, win_send, win_recv, own_in, own_out,
):
    ctx, head = lax.axis_index("ctx"), lax.axis_index("head")
    n_ctx, n_head = lax.axis_size("ctx"), lax.axis_size("head")

    def cut(which, j):
        if which == 0:
            return k_in.at[:, pl.ds(pl.multiple_of(j * HEAD_DIM, HEAD_DIM), HEAD_DIM)]
        if which == 1:
            return v_in.at[:, pl.ds(pl.multiple_of(j * HEAD_DIM, HEAD_DIM), HEAD_DIM)]
        if which == 2:
            return nd_in.at[j]
        if which == 3:
            return q_in.at[:, pl.ds(pl.multiple_of(j * WIDTH, WIDTH), WIDTH)]
        return g_in.at[:, pl.ds(pl.multiple_of(j * WIDTH, WIDTH), WIDTH)]

    def place(which, t):
        if which == 0:
            return k_out.at[0, t]
        if which == 1:
            return v_out.at[0, t]
        return (nd_out, q_out, g_out)[which - 2].at[t]

    temps = (k_tmp, v_tmp, nd_tmp, q_tmp, g_tmp)
    loads = [
        pltpu.make_async_copy(cut(w, head), temps[w], own_in.at[w]) for w in range(5)
    ]
    for load in loads:
        load.start()

    greet(ctx, head)

    def copy(which, d):
        j = wrap(head + d, n_head)
        return pltpu.make_async_remote_copy(
            src_ref=cut(which, j),
            dst_ref=place(which, head),
            send_sem=send.at[which, d],
            recv_sem=recv.at[which, d],
            device_id=(ctx, j),
            device_id_type=MESH,
        )

    copies = {(w, d): copy(w, d) for w in range(5) for d in range(1, n_head)}
    for w in (0, 1, 2, 3):
        for d in range(1, n_head):
            copies[w, d].start()
    stores = [
        pltpu.make_async_copy(temps[w], place(w, head), own_out.at[w]) for w in range(5)
    ]
    for w in range(5):
        loads[w].wait()
        stores[w].start()
    windows = []
    for which, out in ((0, k_out), (1, v_out)):
        stores[which].wait()
        for d in range(1, n_head):
            copies[which, d].wait_recv()
        for s in range(1, WIN):
            window = pltpu.make_async_remote_copy(
                src_ref=out.at[0],
                dst_ref=out.at[s],
                send_sem=win_send.at[which, s],
                recv_sem=win_recv.at[which, s],
                device_id=(wrap(ctx + s, n_ctx), head),
                device_id_type=MESH,
            )
            window.start()
            windows.append(window)
    for d in range(1, n_head):
        copies[4, d].start()
    for w in (2, 3, 4):
        stores[w].wait()
        for d in range(1, n_head):
            copies[w, d].wait_recv()
    for window in windows:
        window.wait()
    for one in copies.values():
        one.wait_send()


def gather(q, g, k, v, nd):
    any_spec = pl.BlockSpec(memory_space=pl.ANY)
    bf = jnp.bfloat16
    return pl.pallas_call(
        gather_kernel,
        out_shape=(
            jax.ShapeDtypeStruct((TPB, TILE, WIDTH), bf),
            jax.ShapeDtypeStruct((TPB, TILE, WIDTH), bf),
            jax.ShapeDtypeStruct((WIN, TPB, TILE, HEAD_DIM), bf),
            jax.ShapeDtypeStruct((WIN, TPB, TILE, HEAD_DIM), bf),
            jax.ShapeDtypeStruct((TPB, 2 * GROUP, TILE), jnp.float32),
        ),
        in_specs=[any_spec] * 5,
        out_specs=(any_spec,) * 5,
        scratch_shapes=[
            pltpu.VMEM((TILE, WIDTH), bf),
            pltpu.VMEM((TILE, WIDTH), bf),
            pltpu.VMEM((TILE, HEAD_DIM), bf),
            pltpu.VMEM((TILE, HEAD_DIM), bf),
            pltpu.VMEM((2 * GROUP, TILE), jnp.float32),
            pltpu.SemaphoreType.DMA((5, TPB)),
            pltpu.SemaphoreType.DMA((5, TPB)),
            pltpu.SemaphoreType.DMA((2, WIN)),
            pltpu.SemaphoreType.DMA((2, WIN)),
            pltpu.SemaphoreType.DMA((5,)),
            pltpu.SemaphoreType.DMA((5,)),
        ],
        compiler_params=pltpu.CompilerParams(collective_id=0, has_side_effects=True),
        name="gather_heads",
    )(q, g, k, v, nd)


def attend_kernel(
    pairs, count, q_ref, g_ref, nd_ref, k_ref, v_ref,
    dq_ref, dk0_ref, dv0_ref, dkp_ref, dvp_ref, acc_q, acc_k, acc_v, k_t,
):
    row = lax.broadcasted_iota(jnp.int32, (TILE, 2 * TILE), 0)
    col = lax.broadcasted_iota(jnp.int32, (TILE, 2 * TILE), 1)
    causal = row <= jnp.where(col >= TILE, col - TILE, col)

    def pair(s, qt, kt, first):
        key, value, key_t = k_ref[s, kt], v_ref[s, kt], k_t[kt]
        key_term = value_term = None
        for hp in range(GROUP // 2):
            lo, mid, hi = 2 * hp * HEAD_DIM, (2 * hp + 1) * HEAD_DIM, (2 * hp + 2) * HEAD_DIM
            query = jnp.concatenate([q_ref[qt, :, lo:mid], q_ref[qt, :, mid:hi]], axis=0)
            grad = jnp.concatenate([g_ref[qt, :, lo:mid], g_ref[qt, :, mid:hi]], axis=0)
            norm = jnp.concatenate([nd_ref[qt, 2 * hp : 2 * hp + 1], nd_ref[qt, 2 * hp + 1 : 2 * hp + 2]], axis=1)
            delta = jnp.concatenate([nd_ref[qt, GROUP + 2 * hp : GROUP + 2 * hp + 1], nd_ref[qt, GROUP + 2 * hp + 1 : GROUP + 2 * hp + 2]], axis=1)
            over = (((1,), (1,)), ((), ()))
            scores = lax.dot_general(key, query, over, preferred_element_type=jnp.float32)
            probs = jnp.exp2(scores * (SCALE * LOG2E) - norm)
            if first:
                probs = jnp.where(causal, probs, 0.0)
            prob_grad = lax.dot_general(value, grad, over, preferred_element_type=jnp.float32)
            score_grad = (SCALE * probs * (prob_grad - delta)).astype(jnp.bfloat16)
            low = probs.astype(jnp.bfloat16)
            kterm = jnp.dot(score_grad, query, preferred_element_type=jnp.float32)
            vterm = jnp.dot(low, grad, preferred_element_type=jnp.float32)
            key_term = kterm if key_term is None else key_term + kterm
            value_term = vterm if value_term is None else value_term + vterm
            qterm = jnp.dot(key_t, score_grad, preferred_element_type=jnp.float32)
            if first:
                acc_q[qt, :, lo:hi] = qterm
            else:
                acc_q[qt, :, lo:hi] += qterm
        if first:
            acc_k[kt] = key_term
            acc_v[kt] = value_term
        else:
            acc_k[kt] += key_term
            acc_v[kt] += value_term

    for s in range(WIN):
        @pl.loop(0, TPB)
        def _(t, s=s):
            k_t[t] = k_ref[s, t].T

        if s == 0:
            @pl.loop(0, TPB)
            def _(t):
                pair(0, t, t, True)
        else:
            acc_k[...] = jnp.zeros_like(acc_k)
            acc_v[...] = jnp.zeros_like(acc_v)

        @pl.loop(TPB if s == 0 else 0, count[s])
        def _(slot, s=s):
            pair(s, pairs[(s * SLOTS + slot) * 2], pairs[(s * SLOTS + slot) * 2 + 1], False)

        if s == 0:
            dk0_ref[...] = acc_k[...]
            dv0_ref[...] = acc_v[...]
        else:
            dkp_ref[s - 1] = acc_k[...].astype(jnp.bfloat16)
            dvp_ref[s - 1] = acc_v[...].astype(jnp.bfloat16)

    @pl.loop(0, TPB)
    def _(t):
        for h in range(GROUP):
            at = slice(h * HEAD_DIM, (h + 1) * HEAD_DIM)
            dq_ref[t, :, at] = acc_q[t, :, at].astype(jnp.bfloat16).T


def attend(pairs, count, q, g, nd, k, v):
    bf, f32 = jnp.bfloat16, jnp.float32
    smem = pl.BlockSpec(memory_space=pltpu.SMEM)
    vmem = pl.BlockSpec(memory_space=pltpu.VMEM)
    return pl.pallas_call(
        attend_kernel,
        out_shape=(
            jax.ShapeDtypeStruct((TPB, TILE, WIDTH), bf),
            jax.ShapeDtypeStruct((TPB, TILE, HEAD_DIM), f32),
            jax.ShapeDtypeStruct((TPB, TILE, HEAD_DIM), f32),
            jax.ShapeDtypeStruct((WIN - 1, TPB, TILE, HEAD_DIM), bf),
            jax.ShapeDtypeStruct((WIN - 1, TPB, TILE, HEAD_DIM), bf),
        ),
        in_specs=[smem, smem] + [vmem] * 5,
        out_specs=(vmem,) * 5,
        scratch_shapes=[
            pltpu.VMEM((TPB, HEAD_DIM, WIDTH), f32),
            pltpu.VMEM((TPB, TILE, HEAD_DIM), f32),
            pltpu.VMEM((TPB, TILE, HEAD_DIM), f32),
            pltpu.VMEM((TPB, HEAD_DIM, TILE), bf),
        ],
        name="attend_pairs",
    )(pairs, count, q, g, nd, k, v)


def scatter_kernel(
    dq_in, dk0, dv0, dkp, dvp, dq_out, dk_out, dv_out,
    own, got_k, got_v, sum_k, sum_v, send, recv, win_send, win_recv, own_sem,
):
    ctx, head = lax.axis_index("ctx"), lax.axis_index("head")
    n_ctx, n_head = lax.axis_size("ctx"), lax.axis_size("head")
    load = pltpu.make_async_copy(dq_in.at[head], own, own_sem.at[0])
    load.start()
    greet(ctx, head)
    wide = pl.ds(pl.multiple_of(head * WIDTH, WIDTH), WIDTH)
    slim = pl.ds(pl.multiple_of(head * HEAD_DIM, HEAD_DIM), HEAD_DIM)

    windows = []
    for which, (src, got) in enumerate(((dkp, got_k), (dvp, got_v))):
        for s in range(1, WIN):
            window = pltpu.make_async_remote_copy(
                src_ref=src.at[s - 1],
                dst_ref=got.at[s - 1],
                send_sem=win_send.at[which, s],
                recv_sem=win_recv.at[which, s],
                device_id=(wrap(ctx - s, n_ctx), head),
                device_id_type=MESH,
            )
            window.start()
            windows.append(window)

    def copy(which, d):
        j = wrap(head + d, n_head)
        src = (dq_in, sum_k, sum_v)[which].at[j]
        dst = (dq_out.at[:, wide], dk_out.at[:, slim], dv_out.at[:, slim])[which]
        return pltpu.make_async_remote_copy(
            src_ref=src,
            dst_ref=dst,
            send_sem=send.at[which, d],
            recv_sem=recv.at[which, d],
            device_id=(ctx, j),
            device_id_type=MESH,
        )

    copies = {(w, d): copy(w, d) for w in range(3) for d in range(1, n_head)}
    for d in range(1, n_head):
        copies[0, d].start()
    load.wait()
    own_q = pltpu.make_async_copy(own, dq_out.at[:, wide], own_sem.at[1])
    own_q.start()
    for window in windows:
        window.wait_recv()
    for base, got, total in ((dk0, got_k, sum_k), (dv0, got_v, sum_v)):
        value = base[...]
        for s in range(WIN - 1):
            value = value + got[s].astype(jnp.float32)
        total[...] = value.astype(jnp.bfloat16)
    for d in range(1, n_head):
        copies[1, d].start()
        copies[2, d].start()
    own_k = pltpu.make_async_copy(sum_k.at[head], dk_out.at[:, slim], own_sem.at[2])
    own_v = pltpu.make_async_copy(sum_v.at[head], dv_out.at[:, slim], own_sem.at[3])
    own_k.start()
    own_v.start()
    own_q.wait()
    own_k.wait()
    own_v.wait()
    for one in copies.values():
        one.wait()
    for window in windows:
        window.wait_send()


def scatter(dq, dk0, dv0, dkp, dvp):
    any_spec = pl.BlockSpec(memory_space=pl.ANY)
    vmem = pl.BlockSpec(memory_space=pltpu.VMEM)
    bf = jnp.bfloat16
    return pl.pallas_call(
        scatter_kernel,
        out_shape=(
            jax.ShapeDtypeStruct((TILE, TPB * WIDTH), bf),
            jax.ShapeDtypeStruct((TILE, TPB * HEAD_DIM), bf),
            jax.ShapeDtypeStruct((TILE, TPB * HEAD_DIM), bf),
        ),
        in_specs=[any_spec, vmem, vmem, any_spec, any_spec],
        out_specs=(any_spec,) * 3,
        scratch_shapes=[
            pltpu.VMEM((TILE, WIDTH), bf),
            pltpu.VMEM((WIN - 1, TPB, TILE, HEAD_DIM), bf),
            pltpu.VMEM((WIN - 1, TPB, TILE, HEAD_DIM), bf),
            pltpu.VMEM((TPB, TILE, HEAD_DIM), bf),
            pltpu.VMEM((TPB, TILE, HEAD_DIM), bf),
            pltpu.SemaphoreType.DMA((3, TPB)),
            pltpu.SemaphoreType.DMA((3, TPB)),
            pltpu.SemaphoreType.DMA((2, WIN)),
            pltpu.SemaphoreType.DMA((2, WIN)),
            pltpu.SemaphoreType.DMA((4,)),
        ],
        compiler_params=pltpu.CompilerParams(collective_id=1, has_side_effects=True),
        name="scatter_grads",
    )(dq, dk0, dv0, dkp, dvp)


def per_device(queries, keys, values, out_grad, log_norm, row_delta, tile_pairs, pair_count):
    by_head = jnp.stack([log_norm * LOG2E, row_delta], axis=0)
    by_head = by_head.reshape(2, TILE, TPB, GROUP)
    by_head = jnp.transpose(by_head, (2, 0, 3, 1)).reshape(TPB, 2 * GROUP, TILE)
    q, g, k, v, nd = gather(queries, out_grad, keys, values, by_head)
    grads = attend(tile_pairs.reshape(-1), pair_count.reshape(-1), q, g, nd, k, v)
    return scatter(*grads)


def solution(mesh):
    rows = P(("ctx", "head"), None)
    return jax.shard_map(
        per_device,
        mesh=mesh,
        in_specs=(rows,) * 6 + (P("ctx", None, None, None), P("ctx", None)),
        out_specs=(rows,) * 3,
        check_vma=False,
    )
```

profile of v0, /device:TPU:192, one launch (start us, length us, event | category | flops | bytes accessed | tf_op | source)
XLA Modules:
  0.0 153.7 jit_solution(6421678975431099125)
XLA Ops:
  0.6 0.0 copy-start.2
  0.6 0.7 broadcast_multiply_fusion
  1.4 0.0 copy-done.2
  1.4 0.0 copy-start.3
  1.4 0.6 pad_maximum_fusion
  2.0 0.1 copy-done.3
  2.1 0.1 copy.14
  2.2 0.7 reshape.20.pairs
  2.8 59.6 %gather_heads.1 = (bf16[8,128,512]{2,1,0:T(8,128)(2,1)}, bf16[8,128,512]{2,1,0:T(8,128)(2,1)}, bf16[4,8,128,128]{3,2,1,0:T(8,128)(2,1)}, bf16[4,8,128,128]{3,2,1,0:T(8,128)(2,1)}, f32[8,8,128]{2,1,0:T(8,128)}) custom-call(bf16[128,4096]{1,0:T(8,128)(2,1)} %q_in.1, bf16[128,4096]{1,0:T(8,128)(2,1)} %g_in.1, bf16[128,1024]{1,0:T(8,128)(2,1)} %k_in.1, ...), custom_call_target="tpu_custom_call" | custom-call | tf_op jit(solution)/shard_map/gather_heads/pallas_call | solution.py:125
  62.4 31.1 %attend_pairs.1 = (bf16[8,128,512]{2,1,0:T(8,128)(2,1)}, f32[8,128,128]{2,1,0:T(8,128)}, f32[8,128,128]{2,1,0:T(8,128)}, bf16[3,8,128,128]{3,2,1,0:T(8,128)(2,1)}, bf16[3,8,128,128]{3,2,1,0:T(8,128)(2,1)}) custom-call(s32[128]{0:T(128)} %reshape.20.pairs, s32[4]{0:T(128)} %bitcast.15, bf16[8,128,512]{2,1,0:T(8,128)(2,1)} %get-tuple-element.13.q_ref, ...), custom_call_target="tpu_custom_call" | custom-call | tf_op jit(solution)/shard_map/attend_pairs/pallas_call | solution.py:230
  93.5 56.1 %scatter_grads.1 = (bf16[128,4096]{1,0:T(8,128)(2,1)}, bf16[128,1024]{1,0:T(8,128)(2,1)}, bf16[128,1024]{1,0:T(8,128)(2,1)}) custom-call(bf16[8,128,512]{2,1,0:T(8,128)(2,1)} %get-tuple-element.18.dq_in, f32[8,128,128]{2,1,0:T(8,128)} %get-tuple-element.19.dk0, f32[8,128,128]{2,1,0:T(8,128)} %get-tuple-element.20.dv0, ...), custom_call_target="tpu_custom_call" | custom-call | tf_op jit(solution)/shard_map/scatter_grads/pallas_call | solution.py:323
  149.6 0.0 copy-start.1
  149.6 2.3 %copy.20 = bf16[128,4096]{1,0:T(8,128)(2,1)} copy(bf16[128,4096]{1,0:T(8,128)(2,1)} %get-tuple-element.26) | data formatting | bytes 2097152
  152.0 0.0 copy-done.1
  152.0 0.0 copy-start
  152.0 0.7 copy.21
  152.7 0.3 copy-done
  153.0 0.7 copy.22
Async XLA Ops:
  0.6 0.7 copy-start.2
  1.4 0.7 copy-start.3
  149.6 2.3 %copy-start.1 = (bf16[128,1024]{1,0:T(8,128)(2,1)S(1)}, bf16[128,1024]{1,0:T(8,128)(2,1)}, u32[]{:S(2)}) copy-start(bf16[128,1024]{1,0:T(8,128)(2,1)} %get-tuple-element.27) | copy-start | bytes 786436
  152.0 1.0 copy-start
where the time goes:
time: 154 us
  Pallas kernels  147 us (95%)
  local copies, waits for them, and re-layouts  4.9 us (3%)
    pallas_call x1, Pallas kernels, gather(): pl.pallas_call(gather_kernel, out_shape=(jax.ShapeDtypeStruct((TPB, TILE,...  59.6 us
    pallas_call x1, Pallas kernels, scatter(): pl.pallas_call(scatter_kernel, out_shape=(jax.ShapeDtypeStruct((TILE, TPB...  56.1 us
    pallas_call x1, Pallas kernels, attend(): pl.pallas_call(attend_kernel, out_shape=(jax.ShapeDtypeStruct((TPB, TILE,...  31.1 us
    unnamed x12, local copies, waits for them, and re-layouts  4.25 us

commit v1 on v0

--- a/solution.py
+++ b/solution.py
@@ -91,30 +91,63 @@
     for w in range(5):
         loads[w].wait()
         stores[w].start()
-    windows = []
-    for which, out in ((0, k_out), (1, v_out)):
+    def window(which, source, s, slot, hop):
+        out = (k_out, v_out)[which]
+        return pltpu.make_async_remote_copy(
+            src_ref=out.at[source],
+            dst_ref=out.at[s],
+            send_sem=win_send.at[which, slot],
+            recv_sem=win_recv.at[which, s],
+            device_id=(wrap(ctx + hop, n_ctx), head),
+            device_id_type=MESH,
+        )
+
+    even = lax.rem(ctx, 2) == 0
+    for which in (0, 1):
         stores[which].wait()
         for d in range(1, n_head):
             copies[which, d].wait_recv()
-        for s in range(1, WIN):
-            window = pltpu.make_async_remote_copy(
-                src_ref=out.at[0],
-                dst_ref=out.at[s],
-                send_sem=win_send.at[which, s],
-                recv_sem=win_recv.at[which, s],
-                device_id=(wrap(ctx + s, n_ctx), head),
-                device_id_type=MESH,
-            )
-            window.start()
-            windows.append(window)
+
+        @pl.when(even)
+        def _(which=which):
+            window(which, 0, 2, 1, 2).start()
+            window(which, 0, 1, 0, 1).start()
+
+        @pl.when(jnp.logical_not(even))
+        def _(which=which):
+            window(which, 0, 1, 0, 1).start()
+            window(which, 0, 3, 1, 3).start()
+
     for d in range(1, n_head):
         copies[4, d].start()
+
+    @pl.when(even)
+    def _():
+        for which in (0, 1):
+            window(which, 0, 1, 0, 1).wait_recv()
+            window(which, 1, 2, 2, 1).start()
+        for which in (0, 1):
+            window(which, 0, 2, 0, 1).wait_recv()
+            window(which, 2, 3, 3, 1).start()
+        for which in (0, 1):
+            window(which, 0, 3, 0, 1).wait_recv()
+            window(which, 0, 2, 1, 2).wait_send()
+            window(which, 0, 1, 0, 1).wait_send()
+            window(which, 1, 2, 2, 1).wait_send()
+            window(which, 2, 3, 3, 1).wait_send()
+
+    @pl.when(jnp.logical_not(even))
+    def _():
+        for which in (0, 1):
+            for s in range(1, WIN):
+                window(which, 0, s, 0, 1).wait_recv()
+            window(which, 0, 1, 0, 1).wait_send()
+            window(which, 0, 3, 1, 3).wait_send()
+
     for w in (2, 3, 4):
         stores[w].wait()
         for d in range(1, n_head):
             copies[w, d].wait_recv()
-    for window in windows:
-        window.wait()
     for one in copies.values():
         one.wait_send()
 
@@ -250,7 +283,7 @@
 
 def scatter_kernel(
     dq_in, dk0, dv0, dkp, dvp, dq_out, dk_out, dv_out,
-    own, got_k, got_v, sum_k, sum_v, send, recv, win_send, win_recv, own_sem,
+    own, got_k, got_v, add_k, add_v, tmp_k, tmp_v, sum_k, sum_v, send, recv, win_send, win_recv, own_sem,
 ):
     ctx, head = lax.axis_index("ctx"), lax.axis_index("head")
     n_ctx, n_head = lax.axis_size("ctx"), lax.axis_size("head")
@@ -260,19 +293,40 @@
     wide = pl.ds(pl.multiple_of(head * WIDTH, WIDTH), WIDTH)
     slim = pl.ds(pl.multiple_of(head * HEAD_DIM, HEAD_DIM), HEAD_DIM)
 
-    windows = []
-    for which, (src, got) in enumerate(((dkp, got_k), (dvp, got_v))):
-        for s in range(1, WIN):
-            window = pltpu.make_async_remote_copy(
-                src_ref=src.at[s - 1],
-                dst_ref=got.at[s - 1],
-                send_sem=win_send.at[which, s],
-                recv_sem=win_recv.at[which, s],
-                device_id=(wrap(ctx - s, n_ctx), head),
-                device_id_type=MESH,
-            )
-            window.start()
-            windows.append(window)
+    even = lax.rem(ctx, 2) == 0
+    parts, gots = (dkp, dvp), (got_k, got_v)
+    adds, tmps = (add_k, add_v), (tmp_k, tmp_v)
+
+    def part(which, src, slot, sem, back):
+        return pltpu.make_async_remote_copy(
+            src_ref=src,
+            dst_ref=gots[which].at[slot],
+            send_sem=win_send.at[which, sem],
+            recv_sem=win_recv.at[which, slot],
+            device_id=(wrap(ctx - back, n_ctx), head),
+            device_id_type=MESH,
+        )
+
+    def odd_parts(which):
+        return [part(which, parts[which].at[s], s, s, 1) for s in (1, 2, 0)]
+
+    def even_parts(which):
+        return [
+            part(which, adds[which].at[0], 3, 0, 1),
+            part(which, adds[which].at[1], 4, 1, 2),
+            part(which, parts[which].at[2], 4, 2, 3),
+        ]
+
+    @pl.when(jnp.logical_not(even))
+    def _():
+        for i in range(WIN - 1):
+            for which in (0, 1):
+                odd_parts(which)[i].start()
+
+    @pl.when(even)
+    def _():
+        for which in (0, 1):
+            even_parts(which)[2].start()
 
     def copy(which, d):
         j = wrap(head + d, n_head)
@@ -293,13 +347,43 @@
     load.wait()
     own_q = pltpu.make_async_copy(own, dq_out.at[:, wide], own_sem.at[1])
     own_q.start()
-    for window in windows:
-        window.wait_recv()
-    for base, got, total in ((dk0, got_k, sum_k), (dv0, got_v, sum_v)):
-        value = base[...]
-        for s in range(WIN - 1):
-            value = value + got[s].astype(jnp.float32)
-        total[...] = value.astype(jnp.bfloat16)
+    loads = [
+        pltpu.make_async_copy(parts[which].at[i], tmps[which].at[i], own_sem.at[4 + 2 * which + i])
+        for i in (0, 1)
+        for which in (0, 1)
+    ]
+
+    @pl.when(even)
+    def _():
+        for one in loads:
+            one.start()
+        for one in loads:
+            one.wait()
+        for i in (0, 1):
+            for which in (0, 1):
+                part(which, parts[which].at[0], i + 1, 0, 1).wait_recv()
+                mine = tmps[which][i].astype(jnp.float32)
+                theirs = gots[which][i + 1].astype(jnp.float32)
+                adds[which][i] = (mine + theirs).astype(jnp.bfloat16)
+                even_parts(which)[i].start()
+        for which in (0, 1):
+            part(which, parts[which].at[0], 0, 0, 1).wait_recv()
+            part(which, parts[which].at[0], 4, 0, 1).wait_recv()
+            value = (dk0, dv0)[which][...]
+            value = value + gots[which][0].astype(jnp.float32)
+            value = value + gots[which][4].astype(jnp.float32)
+            (sum_k, sum_v)[which][...] = value.astype(jnp.bfloat16)
+
+    @pl.when(jnp.logical_not(even))
+    def _():
+        for which in (0, 1):
+            part(which, parts[which].at[0], 3, 0, 1).wait_recv()
+            part(which, parts[which].at[0], 4, 0, 1).wait_recv()
+            value = (dk0, dv0)[which][...]
+            value = value + gots[which][3].astype(jnp.float32)
+            value = value + gots[which][4].astype(jnp.float32)
+            (sum_k, sum_v)[which][...] = value.astype(jnp.bfloat16)
+
     for d in range(1, n_head):
         copies[1, d].start()
         copies[2, d].start()
@@ -312,8 +396,18 @@
     own_v.wait()
     for one in copies.values():
         one.wait()
-    for window in windows:
-        window.wait_send()
+
+    @pl.when(even)
+    def _():
+        for which in (0, 1):
+            for one in even_parts(which):
+                one.wait_send()
+
+    @pl.when(jnp.logical_not(even))
+    def _():
+        for which in (0, 1):
+            for one in odd_parts(which):
+                one.wait_send()
 
 
 def scatter(dq, dk0, dv0, dkp, dvp):
@@ -331,15 +425,19 @@
         out_specs=(any_spec,) * 3,
         scratch_shapes=[
             pltpu.VMEM((TILE, WIDTH), bf),
-            pltpu.VMEM((WIN - 1, TPB, TILE, HEAD_DIM), bf),
-            pltpu.VMEM((WIN - 1, TPB, TILE, HEAD_DIM), bf),
+            pltpu.VMEM((5, TPB, TILE, HEAD_DIM), bf),
+            pltpu.VMEM((5, TPB, TILE, HEAD_DIM), bf),
+            pltpu.VMEM((2, TPB, TILE, HEAD_DIM), bf),
+            pltpu.VMEM((2, TPB, TILE, HEAD_DIM), bf),
+            pltpu.VMEM((2, TPB, TILE, HEAD_DIM), bf),
+            pltpu.VMEM((2, TPB, TILE, HEAD_DIM), bf),
             pltpu.VMEM((TPB, TILE, HEAD_DIM), bf),
             pltpu.VMEM((TPB, TILE, HEAD_DIM), bf),
             pltpu.SemaphoreType.DMA((3, TPB)),
             pltpu.SemaphoreType.DMA((3, TPB)),
             pltpu.SemaphoreType.DMA((2, WIN)),
-            pltpu.SemaphoreType.DMA((2, WIN)),
-            pltpu.SemaphoreType.DMA((4,)),
+            pltpu.SemaphoreType.DMA((2, 5)),
+            pltpu.SemaphoreType.DMA((8,)),
         ],
         compiler_params=pltpu.CompilerParams(collective_id=1, has_side_effects=True),
         name="scatter_grads",

time: 154 us -> 136 us (0.88)
  the two profiles are of different devices: /device:TPU:192 before, /device:TPU:1 now
where the time goes in v1:
time: 136 us; the launch traced here: 135 us
  Pallas kernels  128 us (94%)
  local copies, waits for them, and re-layouts  4.9 us (4%)
    pallas_call x1, Pallas kernels, gather(): pl.pallas_call(gather_kernel, out_shape=(jax.ShapeDtypeStruct((TPB, TILE,...  56.5 us
    pallas_call x1, Pallas kernels, scatter(): pl.pallas_call(scatter_kernel, out_shape=(jax.ShapeDtypeStruct((TILE, TPB...  47.8 us
    pallas_call x1, Pallas kernels, attend(): pl.pallas_call(attend_kernel, out_shape=(jax.ShapeDtypeStruct((TPB, TILE,...  23.5 us
    unnamed x12, local copies, waits for them, and re-layouts  4.25 us

profile of v1, /device:TPU:1, one launch (start us, length us, event | category | flops | bytes accessed | tf_op | source)
XLA Modules:
  0.0 134.7 jit_solution(429519278307214150)
XLA Ops:
  0.6 0.0 copy-start.2
  0.6 0.7 broadcast_multiply_fusion
  1.4 0.0 copy-done.2
  1.4 0.0 copy-start.3
  1.4 0.6 pad_maximum_fusion
  2.0 0.1 copy-done.3
  2.1 0.1 copy.14
  2.2 0.7 reshape.20.pairs
  2.8 56.5 %gather_heads.1 = (bf16[8,128,512]{2,1,0:T(8,128)(2,1)}, bf16[8,128,512]{2,1,0:T(8,128)(2,1)}, bf16[4,8,128,128]{3,2,1,0:T(8,128)(2,1)}, bf16[4,8,128,128]{3,2,1,0:T(8,128)(2,1)}, f32[8,8,128]{2,1,0:T(8,128)}) custom-call(bf16[128,4096]{1,0:T(8,128)(2,1)} %q_in.1, bf16[128,4096]{1,0:T(8,128)(2,1)} %g_in.1, bf16[128,1024]{1,0:T(8,128)(2,1)} %k_in.1, ...), custom_call_target="tpu_custom_call" | custom-call | tf_op jit(solution)/shard_map/gather_heads/pallas_call | solution.py:158
  59.3 23.5 %attend_pairs.1 = (bf16[8,128,512]{2,1,0:T(8,128)(2,1)}, f32[8,128,128]{2,1,0:T(8,128)}, f32[8,128,128]{2,1,0:T(8,128)}, bf16[3,8,128,128]{3,2,1,0:T(8,128)(2,1)}, bf16[3,8,128,128]{3,2,1,0:T(8,128)(2,1)}) custom-call(s32[128]{0:T(128)} %reshape.20.pairs, s32[4]{0:T(128)} %bitcast.15, bf16[8,128,512]{2,1,0:T(8,128)(2,1)} %get-tuple-element.13.q_ref, ...), custom_call_target="tpu_custom_call" | custom-call | tf_op jit(solution)/shard_map/attend_pairs/pallas_call | solution.py:263
  82.8 47.8 %scatter_grads.1 = (bf16[128,4096]{1,0:T(8,128)(2,1)}, bf16[128,1024]{1,0:T(8,128)(2,1)}, bf16[128,1024]{1,0:T(8,128)(2,1)}) custom-call(bf16[8,128,512]{2,1,0:T(8,128)(2,1)} %get-tuple-element.18.dq_in, f32[8,128,128]{2,1,0:T(8,128)} %get-tuple-element.19.dk0, f32[8,128,128]{2,1,0:T(8,128)} %get-tuple-element.20.dv0, ...), custom_call_target="tpu_custom_call" | custom-call | tf_op jit(solution)/shard_map/scatter_grads/pallas_call | solution.py:417
  130.6 0.0 copy-start.1
  130.6 2.3 %copy.20 = bf16[128,4096]{1,0:T(8,128)(2,1)} copy(bf16[128,4096]{1,0:T(8,128)(2,1)} %get-tuple-element.26) | data formatting | bytes 2097152
  132.9 0.0 copy-done.1
  132.9 0.0 copy-start
  132.9 0.7 copy.21
  133.6 0.3 copy-done
  134.0 0.7 copy.22
Async XLA Ops:
  0.6 0.7 copy-start.2
  1.4 0.7 copy-start.3
  130.6 2.3 %copy-start.1 = (bf16[128,1024]{1,0:T(8,128)(2,1)S(1)}, bf16[128,1024]{1,0:T(8,128)(2,1)}, u32[]{:S(2)}) copy-start(bf16[128,1024]{1,0:T(8,128)(2,1)} %get-tuple-element.27) | copy-start | bytes 786436
  132.9 1.0 copy-start

commit v2 on v1

--- a/solution.py
+++ b/solution.py
@@ -12,6 +12,8 @@
 TPB = 8
 WIN = 4
 SLOTS = 16
+PAIRS = 2
+DIAGONALS = 2
 GROUP = 4
 WIDTH = GROUP * HEAD_DIM
 SCALE = HEAD_DIM ** (-0.5)
@@ -186,68 +188,94 @@
 
 def attend_kernel(
     pairs, count, q_ref, g_ref, nd_ref, k_ref, v_ref,
-    dq_ref, dk0_ref, dv0_ref, dkp_ref, dvp_ref, acc_q, acc_k, acc_v, k_t,
+    dq_ref, dk0_ref, dv0_ref, dkp_ref, dvp_ref, acc_q, acc_k, acc_v, k_t, q_list, k_list,
 ):
     row = lax.broadcasted_iota(jnp.int32, (TILE, 2 * TILE), 0)
     col = lax.broadcasted_iota(jnp.int32, (TILE, 2 * TILE), 1)
     causal = row <= jnp.where(col >= TILE, col - TILE, col)
-
-    def pair(s, qt, kt, first):
-        key, value, key_t = k_ref[s, kt], v_ref[s, kt], k_t[kt]
-        key_term = value_term = None
-        for hp in range(GROUP // 2):
-            lo, mid, hi = 2 * hp * HEAD_DIM, (2 * hp + 1) * HEAD_DIM, (2 * hp + 2) * HEAD_DIM
-            query = jnp.concatenate([q_ref[qt, :, lo:mid], q_ref[qt, :, mid:hi]], axis=0)
-            grad = jnp.concatenate([g_ref[qt, :, lo:mid], g_ref[qt, :, mid:hi]], axis=0)
-            norm = jnp.concatenate([nd_ref[qt, 2 * hp : 2 * hp + 1], nd_ref[qt, 2 * hp + 1 : 2 * hp + 2]], axis=1)
-            delta = jnp.concatenate([nd_ref[qt, GROUP + 2 * hp : GROUP + 2 * hp + 1], nd_ref[qt, GROUP + 2 * hp + 1 : GROUP + 2 * hp + 2]], axis=1)
-            over = (((1,), (1,)), ((), ()))
-            scores = lax.dot_general(key, query, over, preferred_element_type=jnp.float32)
-            probs = jnp.exp2(scores * (SCALE * LOG2E) - norm)
-            if first:
+    tiles = WIN * TPB
+    over = (((1,), (1,)), ((), ()))
+
+    def heads(ref, qt, first, n):
+        return jnp.concatenate(
+            [ref[qt, :, h * HEAD_DIM : (h + 1) * HEAD_DIM] for h in range(first, first + n)],
+            axis=0,
+        )
+
+    def row_of(qt, at):
+        return jnp.concatenate([nd_ref[qt, at : at + 1], nd_ref[qt, at + 1 : at + 2]], axis=1)
+
+    def terms(qt, kt, diagonal):
+        key, value = k_ref[kt], v_ref[kt]
+        grads, lows = [], []
+        for at in range(0, GROUP, 2):
+            scores = lax.dot_general(
+                key, heads(q_ref, qt, at, 2), over, preferred_element_type=jnp.float32
+            )
+            prob_grad = lax.dot_general(
+                value, heads(g_ref, qt, at, 2), over, preferred_element_type=jnp.float32
+            )
+            probs = jnp.exp2(scores * (SCALE * LOG2E) - row_of(qt, at))
+            if diagonal:
                 probs = jnp.where(causal, probs, 0.0)
-            prob_grad = lax.dot_general(value, grad, over, preferred_element_type=jnp.float32)
-            score_grad = (SCALE * probs * (prob_grad - delta)).astype(jnp.bfloat16)
-            low = probs.astype(jnp.bfloat16)
-            kterm = jnp.dot(score_grad, query, preferred_element_type=jnp.float32)
-            vterm = jnp.dot(low, grad, preferred_element_type=jnp.float32)
-            key_term = kterm if key_term is None else key_term + kterm
-            value_term = vterm if value_term is None else value_term + vterm
-            qterm = jnp.dot(key_t, score_grad, preferred_element_type=jnp.float32)
-            if first:
-                acc_q[qt, :, lo:hi] = qterm
-            else:
-                acc_q[qt, :, lo:hi] += qterm
-        if first:
-            acc_k[kt] = key_term
-            acc_v[kt] = value_term
-        else:
-            acc_k[kt] += key_term
-            acc_v[kt] += value_term
-
+            score_grad = SCALE * probs * (prob_grad - row_of(qt, GROUP + at))
+            grads.append(score_grad.astype(jnp.bfloat16))
+            lows.append(probs.astype(jnp.bfloat16))
+        score_grad = jnp.concatenate(grads, axis=1)
+        low = jnp.concatenate(lows, axis=1)
+        return (
+            jnp.dot(k_t[kt], score_grad, preferred_element_type=jnp.float32),
+            jnp.dot(score_grad, heads(q_ref, qt, 0, GROUP), preferred_element_type=jnp.float32),
+            jnp.dot(low, heads(g_ref, qt, 0, GROUP), preferred_element_type=jnp.float32),
+        )
+
+    @pl.loop(0, tiles // 4)
+    def _(t):
+        for i in range(4):
+            k_t[4 * t + i] = k_ref[4 * t + i].T
+
+    acc_k[pl.ds(TPB, tiles - TPB + 1)] = jnp.zeros((tiles - TPB + 1, TILE, HEAD_DIM), jnp.float32)
+    acc_v[pl.ds(TPB, tiles - TPB + 1)] = jnp.zeros((tiles - TPB + 1, TILE, HEAD_DIM), jnp.float32)
+    acc_q[TPB] = jnp.zeros((HEAD_DIM, WIDTH), jnp.float32)
+
+    def fill(s, total):
+        first = TPB if s == 0 else 0
+
+        def put(slot, at):
+            q_list[at] = pairs[(s * SLOTS + slot) * 2]
+            k_list[at] = pairs[(s * SLOTS + slot) * 2 + 1] + s * TPB
+            return at + 1
+
+        return lax.fori_loop(first, count[s], put, total)
+
+    total = jnp.int32(0)
     for s in range(WIN):
-        @pl.loop(0, TPB)
-        def _(t, s=s):
-            k_t[t] = k_ref[s, t].T
-
-        if s == 0:
-            @pl.loop(0, TPB)
-            def _(t):
-                pair(0, t, t, True)
-        else:
-            acc_k[...] = jnp.zeros_like(acc_k)
-            acc_v[...] = jnp.zeros_like(acc_v)
-
-        @pl.loop(TPB if s == 0 else 0, count[s])
-        def _(slot, s=s):
-            pair(s, pairs[(s * SLOTS + slot) * 2], pairs[(s * SLOTS + slot) * 2 + 1], False)
-
-        if s == 0:
-            dk0_ref[...] = acc_k[...]
-            dv0_ref[...] = acc_v[...]
-        else:
-            dkp_ref[s - 1] = acc_k[...].astype(jnp.bfloat16)
-            dvp_ref[s - 1] = acc_v[...].astype(jnp.bfloat16)
+        total = fill(s, total)
+    for i in range(PAIRS - 1):
+        q_list[total + i] = TPB
+        k_list[total + i] = tiles
+
+    @pl.loop(0, TPB // DIAGONALS)
+    def _(step):
+        found = [terms(DIAGONALS * step + i, DIAGONALS * step + i, True) for i in range(DIAGONALS)]
+        for i, (query_term, key_term, value_term) in enumerate(found):
+            acc_q[DIAGONALS * step + i] = query_term
+            acc_k[DIAGONALS * step + i] = key_term
+            acc_v[DIAGONALS * step + i] = value_term
+
+    @pl.loop(0, lax.div(total + PAIRS - 1, PAIRS))
+    def _(step):
+        places = [(q_list[PAIRS * step + i], k_list[PAIRS * step + i]) for i in range(PAIRS)]
+        found = [terms(lax.rem(q, TPB), lax.rem(k, tiles), False) for q, k in places]
+        for (q, k), (query_term, key_term, value_term) in zip(places, found):
+            acc_q[q] += query_term
+            acc_k[k] += key_term
+            acc_v[k] += value_term
+
+    dk0_ref[...] = acc_k[pl.ds(0, TPB)]
+    dv0_ref[...] = acc_v[pl.ds(0, TPB)]
+    dkp_ref[...] = acc_k[pl.ds(TPB, tiles - TPB)].astype(jnp.bfloat16)
+    dvp_ref[...] = acc_v[pl.ds(TPB, tiles - TPB)].astype(jnp.bfloat16)
 
     @pl.loop(0, TPB)
     def _(t):
@@ -266,16 +294,18 @@
             jax.ShapeDtypeStruct((TPB, TILE, WIDTH), bf),
             jax.ShapeDtypeStruct((TPB, TILE, HEAD_DIM), f32),
             jax.ShapeDtypeStruct((TPB, TILE, HEAD_DIM), f32),
-            jax.ShapeDtypeStruct((WIN - 1, TPB, TILE, HEAD_DIM), bf),
-            jax.ShapeDtypeStruct((WIN - 1, TPB, TILE, HEAD_DIM), bf),
+            jax.ShapeDtypeStruct(((WIN - 1) * TPB, TILE, HEAD_DIM), bf),
+            jax.ShapeDtypeStruct(((WIN - 1) * TPB, TILE, HEAD_DIM), bf),
         ),
         in_specs=[smem, smem] + [vmem] * 5,
         out_specs=(vmem,) * 5,
         scratch_shapes=[
-            pltpu.VMEM((TPB, HEAD_DIM, WIDTH), f32),
-            pltpu.VMEM((TPB, TILE, HEAD_DIM), f32),
-            pltpu.VMEM((TPB, TILE, HEAD_DIM), f32),
-            pltpu.VMEM((TPB, HEAD_DIM, TILE), bf),
+            pltpu.VMEM((TPB + 1, HEAD_DIM, WIDTH), f32),
+            pltpu.VMEM((WIN * TPB + 1, TILE, HEAD_DIM), f32),
+            pltpu.VMEM((WIN * TPB + 1, TILE, HEAD_DIM), f32),
+            pltpu.VMEM((WIN * TPB, HEAD_DIM, TILE), bf),
+            pltpu.SMEM((WIN * SLOTS + PAIRS,), jnp.int32),
+            pltpu.SMEM((WIN * SLOTS + PAIRS,), jnp.int32),
         ],
         name="attend_pairs",
     )(pairs, count, q, g, nd, k, v)
@@ -449,8 +479,12 @@
     by_head = by_head.reshape(2, TILE, TPB, GROUP)
     by_head = jnp.transpose(by_head, (2, 0, 3, 1)).reshape(TPB, 2 * GROUP, TILE)
     q, g, k, v, nd = gather(queries, out_grad, keys, values, by_head)
-    grads = attend(tile_pairs.reshape(-1), pair_count.reshape(-1), q, g, nd, k, v)
-    return scatter(*grads)
+    tiles = (WIN * TPB, TILE, HEAD_DIM)
+    dq, dk0, dv0, dkp, dvp = attend(
+        tile_pairs.reshape(-1), pair_count.reshape(-1), q, g, nd, k.reshape(tiles), v.reshape(tiles)
+    )
+    parts = (WIN - 1, TPB, TILE, HEAD_DIM)
+    return scatter(dq, dk0, dv0, dkp.reshape(parts), dvp.reshape(parts))
 
 
 def solution(mesh):

time: 136 us -> 126 us (0.926)
  Pallas kernels: 128 us -> 119 us
    pallas_call x1, Pallas kernels: 23.5 us -> 16.9 us  [attend(): pl.pallas_call(attend_kernel, out_shape=(jax.ShapeDtypeStruct((TPB, TILE,...]
    pallas_call x1, Pallas kernels: 47.8 us -> 45.6 us  [scatter(): pl.pallas_call(scatter_kernel, out_shape=(jax.ShapeDtypeStruct((TILE, TPB...]
where the time goes in v2:
time: 126 us
  Pallas kernels  119 us (94%)
  local copies, waits for them, and re-layouts  4.9 us (4%)
  other arithmetic  1.35 us (1%)
    pallas_call x1, Pallas kernels, gather(): pl.pallas_call(gather_kernel, out_shape=(jax.ShapeDtypeStruct((TPB, TILE,...  56.5 us
    pallas_call x1, Pallas kernels, scatter(): pl.pallas_call(scatter_kernel, out_shape=(jax.ShapeDtypeStruct((TILE, TPB...  45.6 us
    pallas_call x1, Pallas kernels, attend(): pl.pallas_call(attend_kernel, out_shape=(jax.ShapeDtypeStruct((TPB, TILE,...  16.9 us
    unnamed x12, local copies, waits for them, and re-layouts  4.25 us

profile of v2, /device:TPU:1, one launch (start us, length us, event | category | flops | bytes accessed | tf_op | source)
XLA Modules:
  0.0 125.8 jit_solution(14231368674815658400)
XLA Ops:
  0.6 0.0 copy-start.2
  0.6 0.7 broadcast_multiply_fusion
  1.4 0.0 copy-done.2
  1.4 0.0 copy-start.3
  1.4 0.6 pad_maximum_fusion
  2.0 0.1 copy-done.3
  2.1 0.1 copy.14
  2.2 0.7 reshape.32.pairs
  2.8 56.5 %gather_heads.1 = (bf16[8,128,512]{2,1,0:T(8,128)(2,1)}, bf16[8,128,512]{2,1,0:T(8,128)(2,1)}, bf16[4,8,128,128]{3,2,1,0:T(8,128)(2,1)}, bf16[4,8,128,128]{3,2,1,0:T(8,128)(2,1)}, f32[8,8,128]{2,1,0:T(8,128)}) custom-call(bf16[128,4096]{1,0:T(8,128)(2,1)} %q_in.1, bf16[128,4096]{1,0:T(8,128)(2,1)} %g_in.1, bf16[128,1024]{1,0:T(8,128)(2,1)} %k_in.1, ...), custom_call_target="tpu_custom_call" | custom-call | tf_op jit(solution)/shard_map/gather_heads/pallas_call | solution.py:160
  59.3 16.9 %attend_pairs.1 = (bf16[8,128,512]{2,1,0:T(8,128)(2,1)}, f32[8,128,128]{2,1,0:T(8,128)}, f32[8,128,128]{2,1,0:T(8,128)}, bf16[24,128,128]{2,1,0:T(8,128)(2,1)}, bf16[24,128,128]{2,1,0:T(8,128)(2,1)}) custom-call(s32[128]{0:T(128)} %reshape.32.pairs, s32[4]{0:T(128)} %bitcast.23, bf16[8,128,512]{2,1,0:T(8,128)(2,1)} %get-tuple-element.13.q_ref, ...), custom_call_target="tpu_custom_call" | custom-call | tf_op jit(solution)/shard_map/attend_pairs/pallas_call | solution.py:291
  76.1 45.6 %scatter_grads.1 = (bf16[128,4096]{1,0:T(8,128)(2,1)}, bf16[128,1024]{1,0:T(8,128)(2,1)}, bf16[128,1024]{1,0:T(8,128)(2,1)}) custom-call(bf16[8,128,512]{2,1,0:T(8,128)(2,1)} %get-tuple-element.18.dq_in, f32[8,128,128]{2,1,0:T(8,128)} %get-tuple-element.19.dk0, f32[8,128,128]{2,1,0:T(8,128)} %get-tuple-element.20.dv0, bf16[3,8,128,128]{3,2,1,0:T(8,128)(2,1)} %bitcast.18, ...), custom_call_target="tpu_custom_call" | custom-call | tf_op jit(solution)/shard_map/scatter_grads/pallas_call | solution.py:447
  121.7 0.0 copy-start.1
  121.7 2.3 %copy.20 = bf16[128,4096]{1,0:T(8,128)(2,1)} copy(bf16[128,4096]{1,0:T(8,128)(2,1)} %get-tuple-element.26) | data formatting | bytes 2097152
  124.0 0.0 copy-done.1
  124.1 0.0 copy-start
  124.1 0.7 copy.21
  124.8 0.3 copy-done
  125.1 0.7 copy.22
Async XLA Ops:
  0.6 0.7 copy-start.2
  1.4 0.7 copy-start.3
  121.7 2.3 %copy-start.1 = (bf16[128,1024]{1,0:T(8,128)(2,1)S(1)}, bf16[128,1024]{1,0:T(8,128)(2,1)}, u32[]{:S(2)}) copy-start(bf16[128,1024]{1,0:T(8,128)(2,1)} %get-tuple-element.27) | copy-start | bytes 786436
  124.1 1.0 copy-start

commit v3 on v2

--- a/solution.py
+++ b/solution.py
@@ -25,7 +25,7 @@
     return lax.rem(value + size, size)
 
 
-def greet(ctx, head):
+def greet(ctx, head, fan=False):
     n_ctx, n_head = lax.axis_size("ctx"), lax.axis_size("head")
     barrier = pltpu.get_barrier_semaphore()
     for d in range(1, n_head):
@@ -35,12 +35,27 @@
     for s in range(1, WIN):
         for there in (wrap(ctx + s, n_ctx), wrap(ctx - s, n_ctx)):
             pl.semaphore_signal(barrier, inc=1, device_id=(there, head), device_id_type=MESH)
-    pl.semaphore_wait(barrier, n_head - 1 + 2 * (WIN - 1))
+    extra = 0
+    if fan:
+        extra = n_head - 1
+
+        @pl.when(lax.rem(ctx, 2) == 0)
+        def _():
+            for d in range(1, n_head):
+                for back in (1, 2):
+                    pl.semaphore_signal(
+                        barrier,
+                        inc=1,
+                        device_id=(wrap(ctx - back, n_ctx), wrap(head + d, n_head)),
+                        device_id_type=MESH,
+                    )
+
+    pl.semaphore_wait(barrier, n_head - 1 + 2 * (WIN - 1) + extra)
 
 
 def gather_kernel(
     q_in, g_in, k_in, v_in, nd_in, q_out, g_out, k_out, v_out, nd_out,
-    q_tmp, g_tmp, k_tmp, v_tmp, nd_tmp, send, recv, win_send, win_recv, own_in, own_out,
+    q_tmp, g_tmp, k_tmp, v_tmp, nd_tmp, send, recv, fan_send, fan_recv, win_send, win_recv, own_in, own_out,
 ):
     ctx, head = lax.axis_index("ctx"), lax.axis_index("head")
     n_ctx, n_head = lax.axis_size("ctx"), lax.axis_size("head")
@@ -70,7 +85,7 @@
     for load in loads:
         load.start()
 
-    greet(ctx, head)
+    greet(ctx, head, fan=True)
 
     def copy(which, d):
         j = wrap(head + d, n_head)
@@ -84,7 +99,26 @@
         )
 
     copies = {(w, d): copy(w, d) for w in range(5) for d in range(1, n_head)}
-    for w in (0, 1, 2, 3):
+    even = lax.rem(ctx, 2) == 0
+    reach = 2 - lax.rem(ctx, 2)
+
+    def fan(which, d, slot):
+        j = wrap(head + d, n_head)
+        return pltpu.make_async_remote_copy(
+            src_ref=cut(which, j),
+            dst_ref=(k_out, v_out)[which].at[slot, head],
+            send_sem=fan_send.at[which, d],
+            recv_sem=fan_recv.at[which, slot, d],
+            device_id=(wrap(ctx + reach, n_ctx), j),
+            device_id_type=MESH,
+        )
+
+    for w in (0, 1):
+        for d in range(1, n_head):
+            copies[w, d].start()
+            fan(w, d, reach).start()
+        fan(w, 0, reach).start()
+    for w in (2, 3):
         for d in range(1, n_head):
             copies[w, d].start()
     stores = [
@@ -104,7 +138,6 @@
             device_id_type=MESH,
         )
 
-    even = lax.rem(ctx, 2) == 0
     for which in (0, 1):
         stores[which].wait()
         for d in range(1, n_head):
@@ -112,12 +145,10 @@
 
         @pl.when(even)
         def _(which=which):
-            window(which, 0, 2, 1, 2).start()
             window(which, 0, 1, 0, 1).start()
 
         @pl.when(jnp.logical_not(even))
         def _(which=which):
-            window(which, 0, 1, 0, 1).start()
             window(which, 0, 3, 1, 3).start()
 
     for d in range(1, n_head):
@@ -126,14 +157,15 @@
     @pl.when(even)
     def _():
         for which in (0, 1):
-            window(which, 0, 1, 0, 1).wait_recv()
+            for d in range(n_head):
+                fan(which, d, 1).wait_recv()
             window(which, 1, 2, 2, 1).start()
         for which in (0, 1):
-            window(which, 0, 2, 0, 1).wait_recv()
+            for d in range(n_head):
+                fan(which, d, 2).wait_recv()
             window(which, 2, 3, 3, 1).start()
         for which in (0, 1):
             window(which, 0, 3, 0, 1).wait_recv()
-            window(which, 0, 2, 1, 2).wait_send()
             window(which, 0, 1, 0, 1).wait_send()
             window(which, 1, 2, 2, 1).wait_send()
             window(which, 2, 3, 3, 1).wait_send()
@@ -143,7 +175,6 @@
         for which in (0, 1):
             for s in range(1, WIN):
                 window(which, 0, s, 0, 1).wait_recv()
-            window(which, 0, 1, 0, 1).wait_send()
             window(which, 0, 3, 1, 3).wait_send()
 
     for w in (2, 3, 4):
@@ -152,6 +183,9 @@
             copies[w, d].wait_recv()
     for one in copies.values():
         one.wait_send()
+    for w in (0, 1):
+        for d in range(n_head):
+            fan(w, d, reach).wait_send()
 
 
 def gather(q, g, k, v, nd):
@@ -176,6 +210,8 @@
             pltpu.VMEM((2 * GROUP, TILE), jnp.float32),
             pltpu.SemaphoreType.DMA((5, TPB)),
             pltpu.SemaphoreType.DMA((5, TPB)),
+            pltpu.SemaphoreType.DMA((2, TPB)),
+            pltpu.SemaphoreType.DMA((2, WIN, TPB)),
             pltpu.SemaphoreType.DMA((2, WIN)),
             pltpu.SemaphoreType.DMA((2, WIN)),
             pltpu.SemaphoreType.DMA((5,)),

time: 126 us -> 122 us (0.968)
  Pallas kernels: 119 us -> 115 us
    pallas_call x1, Pallas kernels: 56.5 us -> 52.5 us  [gather(): pl.pallas_call(gather_kernel, out_shape=(jax.ShapeDtypeStruct((TPB, TILE,...]
where the time goes in v3:
time: 122 us
  Pallas kernels  115 us (94%)
  local copies, waits for them, and re-layouts  4.9 us (4%)
  other arithmetic  1.35 us (1%)
    pallas_call x1, Pallas kernels, gather(): pl.pallas_call(gather_kernel, out_shape=(jax.ShapeDtypeStruct((TPB, TILE,...  52.5 us
    pallas_call x1, Pallas kernels, scatter(): pl.pallas_call(scatter_kernel, out_shape=(jax.ShapeDtypeStruct((TILE, TPB...  46 us
    pallas_call x1, Pallas kernels, attend(): pl.pallas_call(attend_kernel, out_shape=(jax.ShapeDtypeStruct((TPB, TILE,...  16.9 us
    unnamed x12, local copies, waits for them, and re-layouts  4.25 us

profile of v3, /device:TPU:1, one launch (start us, length us, event | category | flops | bytes accessed | tf_op | source)
XLA Modules:
  0.0 122.3 jit_solution(10889421780678153091)
XLA Ops:
  0.6 0.0 copy-start.2
  0.6 0.7 broadcast_multiply_fusion
  1.4 0.0 copy-done.2
  1.4 0.0 copy-start.3
  1.4 0.6 pad_maximum_fusion
  2.0 0.1 copy-done.3
  2.1 0.1 copy.14
  2.2 0.7 reshape.32.pairs
  2.8 52.5 %gather_heads.1 = (bf16[8,128,512]{2,1,0:T(8,128)(2,1)}, bf16[8,128,512]{2,1,0:T(8,128)(2,1)}, bf16[4,8,128,128]{3,2,1,0:T(8,128)(2,1)}, bf16[4,8,128,128]{3,2,1,0:T(8,128)(2,1)}, f32[8,8,128]{2,1,0:T(8,128)}) custom-call(bf16[128,4096]{1,0:T(8,128)(2,1)} %q_in.1, bf16[128,4096]{1,0:T(8,128)(2,1)} %g_in.1, bf16[128,1024]{1,0:T(8,128)(2,1)} %k_in.1, ...), custom_call_target="tpu_custom_call" | custom-call | tf_op jit(solution)/shard_map/gather_heads/pallas_call | solution.py:194
  55.3 16.9 %attend_pairs.1 = (bf16[8,128,512]{2,1,0:T(8,128)(2,1)}, f32[8,128,128]{2,1,0:T(8,128)}, f32[8,128,128]{2,1,0:T(8,128)}, bf16[24,128,128]{2,1,0:T(8,128)(2,1)}, bf16[24,128,128]{2,1,0:T(8,128)(2,1)}) custom-call(s32[128]{0:T(128)} %reshape.32.pairs, s32[4]{0:T(128)} %bitcast.23, bf16[8,128,512]{2,1,0:T(8,128)(2,1)} %get-tuple-element.13.q_ref, ...), custom_call_target="tpu_custom_call" | custom-call | tf_op jit(solution)/shard_map/attend_pairs/pallas_call | solution.py:327
  72.2 46.0 %scatter_grads.1 = (bf16[128,4096]{1,0:T(8,128)(2,1)}, bf16[128,1024]{1,0:T(8,128)(2,1)}, bf16[128,1024]{1,0:T(8,128)(2,1)}) custom-call(bf16[8,128,512]{2,1,0:T(8,128)(2,1)} %get-tuple-element.18.dq_in, f32[8,128,128]{2,1,0:T(8,128)} %get-tuple-element.19.dk0, f32[8,128,128]{2,1,0:T(8,128)} %get-tuple-element.20.dv0, bf16[3,8,128,128]{3,2,1,0:T(8,128)(2,1)} %bitcast.18, ...), custom_call_target="tpu_custom_call" | custom-call | tf_op jit(solution)/shard_map/scatter_grads/pallas_call | solution.py:483
  118.2 0.0 copy-start.1
  118.2 2.3 %copy.20 = bf16[128,4096]{1,0:T(8,128)(2,1)} copy(bf16[128,4096]{1,0:T(8,128)(2,1)} %get-tuple-element.26) | data formatting | bytes 2097152
  120.5 0.0 copy-done.1
  120.5 0.0 copy-start
  120.5 0.7 copy.21
  121.2 0.3 copy-done
  121.6 0.7 copy.22
Async XLA Ops:
  0.6 0.7 copy-start.2
  1.4 0.7 copy-start.3
  118.2 2.3 %copy-start.1 = (bf16[128,1024]{1,0:T(8,128)(2,1)S(1)}, bf16[128,1024]{1,0:T(8,128)(2,1)}, u32[]{:S(2)}) copy-start(bf16[128,1024]{1,0:T(8,128)(2,1)} %get-tuple-element.27) | copy-start | bytes 786436
  120.5 1.0 copy-start
